TPU v7x, 512 devices: a whole 4x4x16 slice. The times are simulated.
512 devices in a mesh: seq: 64 (over z, x), head: 8 (over y, core).
Axes of the slice: x: 4, y: 4, z: 16, core: 2. Of those that a mesh axis runs over, the one named last changes fastest.
Arguments:
- tokens: bfloat16 [8192, 4096], P('seq', 'head')
- gain: float32 [4096], replicated, may hold values from 0.25 to 1.75
- w_query: bfloat16 [4096, 2048], P('seq', 'head'), may hold values from -0.09375 to 0.09375
- w_key: bfloat16 [4096, 2048], P('seq', 'head'), may hold values from -0.09375 to 0.09375
- w_value: bfloat16 [4096, 2048], P('seq', 'head'), may hold values from -0.09375 to 0.09375
- w_out: bfloat16 [2048, 4096], P('head', 'seq'), may hold values from -0.125 to 0.125
- mem_query: bfloat16 [128, 2048], P(None, 'head'), may hold values from -12 to 12
- score_scale: float32 [16], P('head'), may hold values from 1.5 to 4
- decay: float32 [64, 16], P('seq', 'head'), may hold values from 0 to 1, as said below
- seg_len: int32 [64], P('seq'), may hold values from 32 to 128, as said below
Outputs:
- branch: bfloat16 [8192, 4096], P('seq', 'head')
Inputs may be any that keep to these rules, and one draw needn't show every extreme that they name: `decay`: retention lies strictly between 0 and 1. `seg_len`: at least one segment is full and at least one holds exactly 32 valid tokens.
All inputs are finite; a program needn't handle non-finite values.
Results may differ from a plain program's by a relative error of at most 0.015.
Values may be sent and summed in bfloat16 or wider, within the bound.
A program may use at most 64 MiB of HBM per device.

v0:
```python
import math
import jax
import jax.numpy as jnp
from jax import lax
from jax.sharding import PartitionSpec as P

DH = 128


def carried_in(part, axis, combine, identity):
    place = lax.axis_index(axis)
    gathered = jax.tree.map(lambda a: lax.all_gather(a, axis), part)
    state = jax.tree.map(lambda a, e: jnp.zeros_like(a) + jnp.asarray(e, a.dtype), part, identity)

    def one(lap, state):
        return combine(
            state, jax.tree.map(lambda a: lax.dynamic_index_in_dim(a, lap, 0, False), gathered)
        )

    return lax.fori_loop(0, place, one, state)


def body(tokens, gain, w_query, w_key, w_value, w_out, mem_query, score_scale, decay, seg_len):
    seg_rows, feat_local = tokens.shape
    col_local = w_query.shape[1]
    head_size = DH
    heads_local = col_local // head_size
    slot_count = mem_query.shape[0]
    valid_len = seg_len[0]
    inverse_root_scale = 1.0 / math.sqrt(head_size)
    score_bias = math.log(slot_count + seg_rows)
    whole = lax.all_gather(tokens, "head", axis=1, tiled=True)
    wide = whole.astype(jnp.float32)
    mean_squares = jnp.mean(wide * wide, axis=1, keepdims=True)
    normed = (wide * lax.rsqrt(mean_squares + 1e-05) * gain).astype(jnp.bfloat16)
    pieces = (
        lax.all_gather(w_query, "seq", axis=0, tiled=True),
        lax.all_gather(w_key, "seq", axis=0, tiled=True),
        lax.all_gather(w_value, "seq", axis=0, tiled=True),
    )
    query_sum, key_sum, value_sum = tuple(
        (jnp.dot(normed, piece, preferred_element_type=jnp.float32) for piece in pieces)
    )
    query_head_split = query_sum.astype(jnp.bfloat16).reshape(seg_rows, heads_local, head_size)
    key_head_split = key_sum.astype(jnp.bfloat16).reshape(seg_rows, heads_local, head_size)
    value_head_split = value_sum.astype(jnp.bfloat16).reshape(seg_rows, heads_local, head_size)
    positions = jnp.arange(seg_rows, dtype=jnp.int32)
    valid_keys = (positions < valid_len).astype(jnp.float32)
    memory_head_split = mem_query.reshape(slot_count, heads_local, head_size)
    memory_write_scores = (
        jnp.einsum(
            "bia,sia->ibs", memory_head_split, key_head_split, preferred_element_type=jnp.float32
        )
        * inverse_root_scale
    )
    memory_write_weights = (
        jax.nn.sigmoid(memory_write_scores - math.log(seg_rows)) * valid_keys[None, None, :]
    ).astype(jnp.bfloat16)
    memory_written_keys = jnp.einsum(
        "elz,zek->lek", memory_write_weights, key_head_split, preferred_element_type=jnp.float32
    )
    memory_written_values = jnp.einsum(
        "elz,zek->lek", memory_write_weights, value_head_split, preferred_element_type=jnp.float32
    )
    written = jnp.stack(
        [
            memory_written_keys.reshape(slot_count, col_local),
            memory_written_values.reshape(slot_count, col_local),
        ]
    )

    def combine_state(earlier, later):
        return (
            earlier[0] * later[0],
            jnp.repeat(later[0], head_size)[None, None, :] * earlier[1] + later[1],
        )

    retain = decay[0]
    identity = (jnp.ones_like(retain), jnp.zeros_like(written))
    _, memory_in = carried_in((retain, written), "seq", combine_state, identity)
    mem_split = memory_in.reshape(2, slot_count, heads_local, head_size)
    memory_unit_rows = (
        mem_split * lax.rsqrt(jnp.mean(jnp.square(mem_split), axis=3, keepdims=True) + 1e-06)
    ).astype(jnp.bfloat16)
    head_scale_factors = (score_scale * inverse_root_scale)[:, None, None]
    memory_score_matrix = (
        jnp.einsum(
            "zul,rul->uzr",
            query_head_split,
            memory_unit_rows[0],
            preferred_element_type=jnp.float32,
        )
        * head_scale_factors
    )
    tok_scores = (
        jnp.einsum(
            "thd,shd->hts", query_head_split, key_head_split, preferred_element_type=jnp.float32
        )
        * head_scale_factors
    )
    allowed = (positions[None, :] <= positions[:, None]).astype(jnp.float32) * valid_keys[None, :]
    memory_attention_weights = jax.nn.sigmoid(memory_score_matrix - score_bias).astype(jnp.bfloat16)
    token_attention_weights = (
        jax.nn.sigmoid(tok_scores - score_bias) * allowed[None, :, :]
    ).astype(jnp.bfloat16)
    attended_output = jnp.einsum(
        "krf,fku->rku",
        memory_attention_weights,
        memory_unit_rows[1],
        preferred_element_type=jnp.float32,
    )
    attended_output = attended_output + jnp.einsum(
        "ymo,oyl->myl",
        token_attention_weights,
        value_head_split,
        preferred_element_type=jnp.float32,
    )
    attended_output = (
        (attended_output * valid_keys[:, None, None])
        .astype(jnp.bfloat16)
        .reshape(seg_rows, col_local)
    )
    partial_rows = jnp.dot(
        attended_output,
        lax.all_gather(w_out, "seq", axis=1, tiled=True),
        preferred_element_type=jnp.float32,
    )
    branch = lax.psum_scatter(
        partial_rows.astype(jnp.bfloat16), "head", scatter_dimension=1, tiled=True
    )
    return branch


def solution(mesh):
    return jax.shard_map(
        body,
        mesh=mesh,
        in_specs=(
            P("seq", "head"),
            P(),
            P("seq", "head"),
            P("seq", "head"),
            P("seq", "head"),
            P("head", "seq"),
            P(None, "head"),
            P("head"),
            P("seq", "head"),
            P("seq"),
        ),
        out_specs=P("seq", "head"),
        check_vma=False,
    )
```

profile of v0, /device:TPU:2, one launch (start us, length us, event | category | flops | bytes accessed | tf_op | source)
XLA Modules:
  0.0 846.3 jit_solution(12068725102322100497)
XLA Ops:
  6.5 0.7 all-gather.9.cloned.1.call-update
  7.3 0.7 all-gather.11.cloned.1.call-update
  8.1 0.7 all-gather.13.cloned.1.call-update
  8.8 0.5 all-gather.15.cloned.1.call-update
  10.0 34.9 %all-gather.9.cloned.1.call-done = bf16[128,4096]{1,0:T(8,128)(2,1)} async-done(((bf16[128,512]{1,0:T(8,128)(2,1)}), bf16[128,4096]{1,0:T(8,128)(2,1)}) %all-gather.9.cloned.1.call-update) | async-done | bytes 1048592 | tf_op jit(solution)/shard_map/all_gather | solution.py:32
  44.9 1.5 fusion
  46.4 141.3 %all-gather.11.cloned.1.call-done = bf16[4096,256]{1,0:T(8,128)(2,1)} async-done(((bf16[64,256]{1,0:T(8,128)(2,1)}), bf16[4096,256]{1,0:T(8,128)(2,1)}) %all-gather.11.cloned.1.call-update) | async-done | bytes 2097168 | tf_op jit(solution)/shard_map/all_gather | solution.py:38
  187.8 2.4 convolution_convert_fusion.3
  190.3 0.2 fusion.24
  190.9 136.7 %all-gather.13.cloned.1.call-done = bf16[4096,256]{1,0:T(8,128)(2,1)} async-done(((bf16[64,256]{1,0:T(8,128)(2,1)}), bf16[4096,256]{1,0:T(8,128)(2,1)}) %all-gather.13.cloned.1.call-update) | async-done | bytes 2097168 | tf_op jit(solution)/shard_map/all_gather | solution.py:39
  327.6 2.1 convolution_convert_fusion.2
  330.1 0.7 pad_maximum_fusion
  330.9 0.5 all-gather.17.cloned.1.call-update
  331.5 72.5 %all-gather.1 = f32[64,1,2]{2,1,0:T(1,128)S(1)} all-gather(f32[1,1,2]{2,1,0:T(1,128)S(1)} %bitcast.76), channel_id=1, replica_groups=mesh['seq'=64,'head'=8] {'seq'}, dimensions={0}, use_global_device_ids=true | all-gather | bytes 520 | tf_op jit(solution)/shard_map/all_gather | solution.py:12
  404.0 63.3 %all-gather.15.cloned.1.call-done = bf16[4096,256]{1,0:T(8,128)(2,1)} async-done(((bf16[64,256]{1,0:T(8,128)(2,1)}), bf16[4096,256]{1,0:T(8,128)(2,1)}) %all-gather.15.cloned.1.call-update) | async-done | bytes 2097168 | tf_op jit(solution)/shard_map/all_gather | solution.py:37
  467.3 2.1 fusion.26
  469.4 189.2 %all-gather.19.cloned.1.call-done = f32[128,128,256]{2,1,0:T(8,128)} async-done(((f32[2,128,256]{2,1,0:T(8,128)}), f32[128,128,256]{2,1,0:T(8,128)}) %all-gather.19.cloned.1.call-update) | async-done | bytes 16777232 | tf_op jit(solution)/shard_map/all_gather | solution.py:12
  658.7 1.2 while.12
  658.8 1.0 bitcast_add_fusion.2
  660.1 0.3 fusion.25
  660.4 0.3 fusion.21
  660.8 138.3 %all-gather.17.cloned.1.call-done = bf16[256,4096]{0,1:T(8,128)(2,1)} async-done(((bf16[256,64]{0,1:T(8,128)(2,1)}), bf16[256,4096]{0,1:T(8,128)(2,1)}) %all-gather.17.cloned.1.call-update) | async-done | bytes 2097168 | tf_op jit(solution)/shard_map/all_gather | solution.py:125
  799.1 3.4 convolution_convert_fusion
  802.5 37.0 %reduce-scatter.2.cloned.1.call-done = bf16[128,512]{1,0:T(8,128)(2,1)} async-done(((bf16[128,4096]{1,0:T(8,128)(2,1)}), bf16[128,512]{1,0:T(8,128)(2,1)}) %reduce-scatter.2.cloned.1.call-update) | async-done | bytes 131088 | tf_op jit(solution)/shard_map/reduce_scatter | solution.py:128
  (36 shorter events, 1.3 us)
Async XLA Ops:
  6.5 183.8 %copy-start = (bf16[128,256]{1,0:T(8,128)(2,1)S(1)}, bf16[128,256]{1,0:T(8,128)(2,1)}, u32[]{:S(2)}) copy-start(bf16[128,256]{1,0:T(8,128)(2,1)} %param.18) | copy-start | bytes 196612
  6.5 38.4 %all-gather.9.cloned.1.call-start = ((), (), s32[]{:S(2)}) async-start(), calls=%async_computation.1 | async-start | bytes 1179648 | tf_op jit(solution)/shard_map/all_gather | solution.py:32
  7.3 180.5 %all-gather.11.cloned.1.call-start = ((), (), s32[]{:S(2)}) async-start(), calls=%async_computation.2 | async-start | bytes 2129920 | tf_op jit(solution)/shard_map/all_gather | solution.py:38
  8.0 319.6 %all-gather.13.cloned.1.call-start = ((), (), s32[]{:S(2)}) async-start(), calls=%async_computation.3 | async-start | bytes 2129920 | tf_op jit(solution)/shard_map/all_gather | solution.py:39
  8.7 458.6 %all-gather.15.cloned.1.call-start = ((), (), s32[]{:S(2)}) async-start(), calls=%async_computation.4 | async-start | bytes 2129920 | tf_op jit(solution)/shard_map/all_gather | solution.py:37
  9.3 649.4 %all-gather.19.cloned.1.call-start = ((), (), s32[]{:S(2)}) async-start(), calls=%async_computation.7 | async-start | bytes 17039360 | tf_op jit(solution)/shard_map/all_gather | solution.py:12
  46.4 281.2 %copy-start.1 = (bf16[128,4096]{1,0:T(8,128)(2,1)S(1)}, bf16[128,4096]{1,0:T(8,128)(2,1)}, u32[]{:S(2)}) copy-start(bf16[128,4096]{1,0:T(8,128)(2,1)} %all-gather.9.cloned.1.call-done) | copy-start | bytes 3145732
  46.4 281.2 %copy-start.3 = (f32[4096]{0:T(1024)S(1)}, f32[4096]{0:T(1024)}, u32[]{:S(2)}) copy-start(f32[4096]{0:T(1024)} %param.13) | copy-start | bytes 49156
  190.9 140.7 %copy-start.2 = (f32[1,2]{1,0:T(1,128)S(1)}, f32[1,2]{1,0:T(1,128)}, u32[]{:S(2)}) copy-start(f32[1,2]{1,0:T(1,128)} %param.20) | copy-start | bytes 28
  190.9 213.1 %copy-start.4 = (f32[2]{0:T(128)S(1)}, f32[2]{0:T(128)}, u32[]{:S(2)}) copy-start(f32[2]{0:T(128)} %param.19) | copy-start | bytes 28
  330.9 468.2 %all-gather.17.cloned.1.call-start = ((), (), s32[]{:S(2)}) async-start(), calls=%async_computation.5 | async-start | bytes 2129920 | tf_op jit(solution)/shard_map/all_gather | solution.py:125
  331.5 508.0 %reduce-scatter.2.cloned.1.call-start = ((), (), s32[]{:S(2)}) async-start(), calls=%async_computation.6 | async-start | bytes 1179648 | tf_op jit(solution)/shard_map/reduce_scatter | solution.py:128
Sparse Core Ops, SparseCore 0:
  9.5 35.3 all-gather.8
  47.8 139.9 all-gather.10
  190.7 136.8 all-gather.12
  330.4 136.8 all-gather.14
  470.1 188.5 all-gather.18
  661.5 137.5 all-gather.16
  802.6 36.8 reduce-scatter.1
where the time goes:
time: 849 us; the launch traced here: 846 us
  waiting for transfers between devices  744 us (88%)
  blocking collectives  72.5 us (9%)
  between operations  14.3 us (2%)
  matrix products  11.3 us (1%)
    all_gather x1, waiting for transfers between devices, carried_in(): gathered = jax.tree.map(lambda a: lax.all_gather(a, axis), part)  189 us
    all_gather x1, waiting for transfers between devices, body(): lax.all_gather(w_key, 'seq', axis=0, tiled=True)  141 us
    all_gather x1, waiting for transfers between devices, body(): lax.all_gather(w_out, 'seq', axis=1, tiled=True)  138 us
    all_gather x1, waiting for transfers between devices, body(): lax.all_gather(w_value, 'seq', axis=0, tiled=True)  137 us
    all_gather x1, blocking collectives, carried_in(): gathered = jax.tree.map(lambda a: lax.all_gather(a, axis), part)  72.5 us
    all_gather x1, waiting for transfers between devices, body(): lax.all_gather(w_query, 'seq', axis=0, tiled=True)  63.3 us
    reduce_scatter x1, waiting for transfers between devices, body(): lax.psum_scatter(partial_rows.astype(jnp.bfloat16), 'head', scatter_dimen...  37 us
    all_gather x1, waiting for transfers between devices, body(): whole = lax.all_gather(tokens, 'head', axis=1, tiled=True)  34.9 us
  transfers between devices with their start and end apart: 7, of which 7 were waited for; matrix products, arithmetic and copies ran while one was open for 1% of the time, Pallas kernels for 0%

commit v1 on v0

--- a/solution.py
+++ b/solution.py
@@ -5,6 +5,12 @@
 from jax.sharding import PartitionSpec as P
 
 DH = 128
+
+
+def run_ticks(m, named_axis, along_dim):
+    return jnp.concatenate(
+        lax.all_to_all(jnp.stack(lax.axis_size(named_axis) * [m]), named_axis, 0, 0), axis=along_dim
+    )
 
 
 def carried_in(part, axis, combine, identity):
@@ -35,7 +41,7 @@
     normed = (wide * lax.rsqrt(mean_squares + 1e-05) * gain).astype(jnp.bfloat16)
     pieces = (
         lax.all_gather(w_query, "seq", axis=0, tiled=True),
-        lax.all_gather(w_key, "seq", axis=0, tiled=True),
+        run_ticks(w_key, "seq", 0),
         lax.all_gather(w_value, "seq", axis=0, tiled=True),
     )
     query_sum, key_sum, value_sum = tuple(

time: 849 us -> 717 us (0.84)
  the two profiles are of different devices: /device:TPU:2 before, /device:TPU:6 now
where the time goes in v1:
time: 717 us; the launch traced here: 715 us
  waiting for transfers between devices  591 us (82%)
  blocking collectives  71.9 us (10%)
  starting transfers between devices  18.9 us (3%)
  between operations  14.3 us (2%)
  matrix products  9.61 us (1%)
    all_gather x1, waiting for transfers between devices, carried_in(): gathered = jax.tree.map(lambda a: lax.all_gather(a, axis), part)  189 us
    all_gather x1, waiting for transfers between devices, body(): lax.all_gather(w_value, 'seq', axis=0, tiled=True)  150 us
    all_gather x1, waiting for transfers between devices, body(): lax.all_gather(w_out, 'seq', axis=1, tiled=True)  137 us
    all_gather x1, blocking collectives, carried_in(): gathered = jax.tree.map(lambda a: lax.all_gather(a, axis), part)  71.9 us
    all_gather x1, waiting for transfers between devices, body(): lax.all_gather(w_query, 'seq', axis=0, tiled=True)  62.5 us
    reduce_scatter x1, waiting for transfers between devices, body(): lax.psum_scatter(partial_rows.astype(jnp.bfloat16), 'head', scatter_dimen...  37.1 us
    all_to_all x1, starting transfers between devices, run_ticks(): lax.all_to_all(jnp.stack(lax.axis_size(named_axis) * [m]), named_axis, 0, 0)  18.7 us
  transfers between devices with their start and end apart: 7, of which 6 were waited for; matrix products, arithmetic and copies ran while one was open for 2% of the time, Pallas kernels for 0%

profile of v1, /device:TPU:6, one launch (start us, length us, event | category | flops | bytes accessed | tf_op | source)
XLA Modules:
  0.0 715.0 jit_solution(3076605806014958207)
XLA Ops:
  6.5 0.7 all-gather.8.cloned.1.call-update
  7.3 2.4 stack.4
  9.6 18.7 %all-to-all-start = ((bf16[64,64,256]{2,1,0:T(8,128)(2,1)}), bf16[64,64,256]{2,1,0:T(8,128)(2,1)S(1)}, u32[]{:S(2)}, u32[]{:S(2)}) async-start(bf16[64,64,256]{2,1,0:T(8,128)(2,1)} %stack.4), calls=%async_computation | async-start | bytes 4194304 | tf_op jit(solution)/shard_map/all_to_all | solution.py:12
  28.4 0.7 all-gather.10.cloned.1.call-update
  29.1 0.7 all-gather.12.cloned.1.call-update
  30.5 14.3 %all-gather.8.cloned.1.call-done = bf16[128,4096]{1,0:T(8,128)(2,1)} async-done(((bf16[128,512]{1,0:T(8,128)(2,1)}), bf16[128,4096]{1,0:T(8,128)(2,1)}) %all-gather.8.cloned.1.call-update) | async-done | bytes 1048592 | tf_op jit(solution)/shard_map/all_gather | solution.py:38
  44.8 1.5 fusion
  46.4 149.6 %all-gather.10.cloned.1.call-done = bf16[4096,256]{1,0:T(8,128)(2,1)} async-done(((bf16[64,256]{1,0:T(8,128)(2,1)}), bf16[4096,256]{1,0:T(8,128)(2,1)}) %all-gather.10.cloned.1.call-update) | async-done | bytes 2097168 | tf_op jit(solution)/shard_map/all_gather | solution.py:45
  196.0 2.4 convolution_convert_fusion.2
  198.5 0.5 convolution_convert_fusion.3
  199.9 0.7 pad_maximum_fusion
  200.7 0.5 all-gather.14.cloned.1.call-update
  201.3 71.9 %all-gather.1 = f32[64,1,2]{2,1,0:T(1,128)S(1)} all-gather(f32[1,1,2]{2,1,0:T(1,128)S(1)} %bitcast.78), channel_id=1, replica_groups=mesh['seq'=64,'head'=8] {'seq'}, dimensions={0}, use_global_device_ids=true | all-gather | bytes 520 | tf_op jit(solution)/shard_map/all_gather | solution.py:18
  273.3 62.5 %all-gather.12.cloned.1.call-done = bf16[4096,256]{1,0:T(8,128)(2,1)} async-done(((bf16[64,256]{1,0:T(8,128)(2,1)}), bf16[4096,256]{1,0:T(8,128)(2,1)}) %all-gather.12.cloned.1.call-update) | async-done | bytes 2097168 | tf_op jit(solution)/shard_map/all_gather | solution.py:43
  335.8 2.1 fusion.26
  337.9 188.7 %all-gather.16.cloned.1.call-done = f32[128,128,256]{2,1,0:T(8,128)} async-done(((f32[2,128,256]{2,1,0:T(8,128)}), f32[128,128,256]{2,1,0:T(8,128)}) %all-gather.16.cloned.1.call-update) | async-done | bytes 16777232 | tf_op jit(solution)/shard_map/all_gather | solution.py:18
  526.6 3.5 while.12
  526.7 1.0 bitcast_add_fusion.2
  527.9 1.0 bitcast_add_fusion.2
  529.1 1.0 bitcast_add_fusion.2
  530.7 0.3 fusion.21
  531.0 136.6 %all-gather.14.cloned.1.call-done = bf16[256,4096]{0,1:T(8,128)(2,1)} async-done(((bf16[256,64]{0,1:T(8,128)(2,1)}), bf16[256,4096]{0,1:T(8,128)(2,1)}) %all-gather.14.cloned.1.call-update) | async-done | bytes 2097168 | tf_op jit(solution)/shard_map/all_gather | solution.py:131
  667.6 3.4 convolution_convert_fusion
  671.0 37.1 %reduce-scatter.2.cloned.1.call-done = bf16[128,512]{1,0:T(8,128)(2,1)} async-done(((bf16[128,4096]{1,0:T(8,128)(2,1)}), bf16[128,512]{1,0:T(8,128)(2,1)}) %reduce-scatter.2.cloned.1.call-update) | async-done | bytes 131088 | tf_op jit(solution)/shard_map/reduce_scatter | solution.py:134
  (42 shorter events, 2.0 us)
Async XLA Ops:
  6.5 192.6 %copy-start = (bf16[128,256]{1,0:T(8,128)(2,1)S(1)}, bf16[128,256]{1,0:T(8,128)(2,1)}, u32[]{:S(2)}) copy-start(bf16[128,256]{1,0:T(8,128)(2,1)} %param.18) | copy-start | bytes 196612
  6.5 38.3 %all-gather.8.cloned.1.call-start = ((), (), s32[]{:S(2)}) async-start(), calls=%async_computation.2 | async-start | bytes 1179648 | tf_op jit(solution)/shard_map/all_gather | solution.py:38
  9.6 186.3 %copy-start.3 = (f32[4096]{0:T(1024)S(1)}, f32[4096]{0:T(1024)}, u32[]{:S(2)}) copy-start(f32[4096]{0:T(1024)} %param.13) | copy-start | bytes 49156
  9.6 188.9 %all-to-all-start = ((bf16[64,64,256]{2,1,0:T(8,128)(2,1)}), bf16[64,64,256]{2,1,0:T(8,128)(2,1)S(1)}, u32[]{:S(2)}, u32[]{:S(2)}) async-start(bf16[64,64,256]{2,1,0:T(8,128)(2,1)} %stack.4), calls=%async_computation | async-start | bytes 4194304 | tf_op jit(solution)/shard_map/all_to_all | solution.py:12
  28.3 167.6 %all-gather.10.cloned.1.call-start = ((), (), s32[]{:S(2)}) async-start(), calls=%async_computation.3 | async-start | bytes 2129920 | tf_op jit(solution)/shard_map/all_gather | solution.py:45
  29.1 306.7 %all-gather.12.cloned.1.call-start = ((), (), s32[]{:S(2)}) async-start(), calls=%async_computation.4 | async-start | bytes 2129920 | tf_op jit(solution)/shard_map/all_gather | solution.py:43
  29.8 496.8 %all-gather.16.cloned.1.call-start = ((), (), s32[]{:S(2)}) async-start(), calls=%async_computation.7 | async-start | bytes 17039360 | tf_op jit(solution)/shard_map/all_gather | solution.py:18
  46.4 152.1 %copy-start.1 = (bf16[128,4096]{1,0:T(8,128)(2,1)S(1)}, bf16[128,4096]{1,0:T(8,128)(2,1)}, u32[]{:S(2)}) copy-start(bf16[128,4096]{1,0:T(8,128)(2,1)} %all-gather.8.cloned.1.call-done) | copy-start | bytes 3145732
  199.0 2.3 copy-start.2
  199.0 74.2 %copy-start.4 = (f32[2]{0:T(128)S(1)}, f32[2]{0:T(128)}, u32[]{:S(2)}) copy-start(f32[2]{0:T(128)} %param.19) | copy-start | bytes 28
  200.7 466.9 %all-gather.14.cloned.1.call-start = ((), (), s32[]{:S(2)}) async-start(), calls=%async_computation.5 | async-start | bytes 2129920 | tf_op jit(solution)/shard_map/all_gather | solution.py:131
  201.3 506.9 %reduce-scatter.2.cloned.1.call-start = ((), (), s32[]{:S(2)}) async-start(), calls=%async_computation.6 | async-start | bytes 1179648 | tf_op jit(solution)/shard_map/reduce_scatter | solution.py:134
Sparse Core Ops, SparseCore 0:
  9.5 35.3 all-gather.7
  47.8 148.1 all-gather.9
  198.9 136.8 all-gather.11
  338.6 187.9 all-gather.15
  529.4 138.1 all-gather.13
  671.1 36.9 reduce-scatter.1
